TPU v7x, 256 devices: a whole 4x4x8 slice. The times are simulated.
256 devices in a mesh: kq: 128 (over x, y, z), band: 2 (over core).
Axes of the slice: x: 4, y: 4, z: 8, core: 2. Of those that a mesh axis runs over, the one named last changes fastest.
Arguments:
- orbitals: bfloat16 [128, 16, 4096], P('kq', 'band'), may hold values from -6 to 6
- screening: bfloat16 [256, 1024, 1024], P('kq'), may hold values from -0.1875 to 0.1875
- pair_k: int32 [256, 2], replicated, may hold values from 0 to 127, as said below
- pair_q: int32 [256], P('kq'), may hold values from 0 to 255, as said below
- gmap: int32 [1024], replicated, may hold values from 0 to 4095, as said below
Outputs:
- exch_field: float32 [128, 16, 4096], P('kq', 'band')
Inputs may be any that keep to these rules, and one draw needn't show every extreme that they name: Rows are grouped by owner: rows o * 2 to (o + 1) * 2 - 1 belong to kq index o, and pair_k[o * 2 + i, s] = (pair_k[i, s] + o) mod 128 for every row i of owner 0 and both columns s. The 2 * 2 k-points of one owner are all different, and those of owner 0 include 128 - 1 and 64. `pair_q`: row i names one of the 2 transfers of owner o = i // 2, namely 2 * o to 2 * o + 1, and each of them in 1 of the owner's rows. `gmap`: all entries differ; 0 and 4095 are among them.
All inputs are finite; a program needn't handle non-finite values.
Results may differ from a plain program's by a relative error of at most 0.007.
Values may be sent and summed in bfloat16 or wider, within the bound.
A program may use at most 128 MiB of HBM per device.

v0:
```python
import math
import jax
import jax.numpy as jnp
from jax import lax
from jax.sharding import PartitionSpec as P

GRID = 16


def cas_table(gmap, grid_side):
    cells = grid_side**3
    points = jnp.arange(cells, dtype=jnp.int32)
    coord_x = points // (grid_side * grid_side)
    coord_y = points // grid_side % grid_side
    coord_z = points % grid_side
    freq_x = gmap // (grid_side * grid_side)
    freq_y = gmap // grid_side % grid_side
    freq_z = gmap % grid_side
    phase = (
        freq_x[:, None] * coord_x[None, :]
        + freq_y[:, None] * coord_y[None, :]
        + freq_z[:, None] * coord_z[None, :]
    ) % grid_side
    angle = phase.astype(jnp.float32) * (2.0 * math.pi / grid_side)
    return (jnp.cos(angle) + jnp.sin(angle)).astype(jnp.bfloat16)


def pair_fields(left_block, right_block, screen_mat, table):
    rows_left = left_block.shape[0]
    rows_right = right_block.shape[0]
    cells = table.shape[1]
    factor = 1.0 / math.sqrt(cells)
    density = (
        left_block.astype(jnp.float32)[:, None, :] * right_block.astype(jnp.float32)[None, :, :]
    ).astype(jnp.bfloat16)
    density = density.reshape(rows_left * rows_right, cells)
    spectrum = lax.dot_general(
        density, table, (((1,), (1,)), ((), ())), preferred_element_type=jnp.float32
    )
    spectrum = (spectrum * factor).astype(jnp.bfloat16)
    screened = jnp.dot(spectrum, screen_mat, preferred_element_type=jnp.float32).astype(
        jnp.bfloat16
    )
    potential = (jnp.dot(screened, table, preferred_element_type=jnp.float32) * factor).astype(
        jnp.bfloat16
    )
    potential = potential.reshape(rows_left, rows_right, cells)
    toward_left = jnp.einsum(
        "mnr,nr->mr", potential, right_block, preferred_element_type=jnp.float32
    )
    toward_right = jnp.einsum(
        "mnr,mr->nr", potential, left_block, preferred_element_type=jnp.float32
    )
    return (toward_left, toward_right)


def shards(orbitals, screening, pair_k, pair_q, gmap):
    owner_index = lax.axis_index("kq")
    pair_count = pair_q.shape[0]
    local_pairs = lax.dynamic_slice_in_dim(pair_k, owner_index * pair_count, pair_count, 0)
    first_points = local_pairs[:, 0]
    second_points = local_pairs[:, 1]
    shard_piece = lax.all_gather(orbitals, "kq", axis=0, tiled=True)
    numbers = jnp.arange(shard_piece.shape[0], dtype=jnp.int32)
    pick_first = (first_points[:, None] == numbers[None, :]).astype(jnp.bfloat16)
    pick_second = (second_points[:, None] == numbers[None, :]).astype(jnp.bfloat16)
    first_add = jnp.einsum(
        "pc,cnr->pnr", pick_first, shard_piece, preferred_element_type=jnp.float32
    )
    second_add = jnp.einsum(
        "pc,cnr->pnr", pick_second, shard_piece, preferred_element_type=jnp.float32
    )
    first_half = first_add.astype(jnp.bfloat16)
    second_half = second_add.astype(jnp.bfloat16)
    first_full = lax.all_gather(first_half, "band", axis=1, tiled=True)
    table = cas_table(gmap, GRID)
    screen_slots = pair_q - owner_index * screening.shape[0]

    def one_pair(operands):
        left_block, right_block, screen_slot = operands
        screen_mat = lax.dynamic_index_in_dim(screening, screen_slot, 0, keepdims=False)
        return pair_fields(left_block, right_block, screen_mat, table)

    toward_first, toward_second = lax.map(one_pair, (first_full, second_half, screen_slots))
    first_share = lax.psum_scatter(
        toward_first.astype(jnp.bfloat16), "band", scatter_dimension=1, tiled=True
    ).astype(jnp.float32)
    numbers = jnp.arange(orbitals.shape[0] * lax.axis_size("kq"), dtype=jnp.int32)
    pick_first = (numbers[:, None] == first_points[None, :]).astype(jnp.float32)
    pick_second = (numbers[:, None] == second_points[None, :]).astype(jnp.float32)
    first_term = jnp.einsum("cp,pnr->cnr", pick_first, first_share, precision=lax.Precision.HIGHEST)
    second_term = jnp.einsum(
        "cp,pnr->cnr", pick_second, toward_second, precision=lax.Precision.HIGHEST
    )
    return lax.psum_scatter(first_term + second_term, "kq", scatter_dimension=0, tiled=True)


def solution(mesh):
    in_specs = (P("kq", "band", None), P("kq", None, None), P(), P("kq"), P())
    out_specs = P("kq", "band", None)
    return jax.shard_map(shards, mesh=mesh, in_specs=in_specs, out_specs=out_specs, check_vma=False)
```

profile of v0, /device:TPU:0, one launch (start us, length us, event | category | flops | bytes accessed | tf_op | source)
XLA Modules:
  0.0 1275.1 jit_solution(6615732303375635659)
XLA Ops:
  6.5 0.7 all-gather.2.cloned.1.call-update
  7.4 0.6 add_select_fusion.4
  8.0 0.6 add_select_fusion.1
  8.6 1.2 broadcast_subtract_fusion
  9.8 0.7 add_select_fusion.5
  10.5 125.8 %all-gather.2.cloned.1.call-done = bf16[128,8,4096]{2,1,0:T(8,128)(2,1)} async-done(((bf16[1,8,4096]{2,1,0:T(8,128)(2,1)}), bf16[128,8,4096]{2,1,0:T(8,128)(2,1)}) %all-gather.2.cloned.1.call-update) | async-done | bytes 8388624 | tf_op jit(solution)/shard_map/all_gather | solution.py:63
  136.4 12.2 fusion.41
  148.7 12.5 fusion.44
  161.1 2.0 all_gather.7
  163.3 322.6 %while.13 = (s32[]{:T(128)}, bf16[2,16,4096]{2,1,0:T(8,128)(2,1)}, f32[2,8,4096]{2,0,1:T(2,128)S(1)}, bf16[2,8,4096]{2,1,0:T(8,128)(2,1)S(1)}, bf16[2,16,4096]{2...) while((s32[]{:T(128)}, bf16[2,16,4096]{2,1,0:T(8,128)(2,1)}, ...), condition=%wide.region_1.2_spmd.clone, body=%wide.region_0.1_spmd.clone.sunk | while | flops 2589425664 | bytes 13951255 | solution.py:84
  177.3 1.3 dynamic_slice.45
  180.5 1.8 fusion.93
  182.3 74.7 %fusion.94 = bf16[128,1024]{1,0:T(8,128)(2,1)} fusion(s32[4096]{0:T(1024)} %get-tuple-element.283, s32[1024]{0:T(1024)S(1)} %get-tuple-element.284, s32[4096]{0:T(1024)} %get-tuple-element.281, s32[1024]{0:T(1024)S(1)} %get-tuple-element.282, s32[4096]{0:T(1024)} %get-tuple-element.279, s32[1024]{0:T(1024)S(1)} %get-tuple-element.280, ...), kind=kOutput, calls=%fused_computation.19.clone.2 | convolution fusion | flops 1427505152 | bytes 2813952 | tf_op jit(solution)/shard_map/while/body/eval_jaxpr/dot_general | solution.py:41
  257.0 72.3 %multiply_reduce_fusion.4 = (bf16[4096,16]{0,1:T(8,128)(2,1)S(1)}, bf16[128,4096]{1,0:T(8,128)(2,1)S(1)}) fusion(f32[4096,8]{0,1:T(8,128)S(1)} %get-tuple-element.234, bf16[128,1024]{1,0:T(8,128)(2,1)} %fusion.94, s32[4096]{0:T(1024)} %get-tuple-element.283, s32[1024]{0:T(1024)S(1)} %get-tuple-element.284, s32[4096]{0:T(1024)} %get-tuple-element.281, ...), kind=kOutput, calls=%fused_computation.15.clone.2 | convolution fusion | flops 1160183808 | bytes 1634304 | tf_op jit(solution)/shard_map/while/body/eval_jaxpr/dot_general | solution.py:44
  329.3 0.2 multiply_reduce_fusion.5
  329.7 1.1 dynamic_update_slice.14
  330.8 0.7 copy-done.3
  331.5 1.3 dynamic_slice.45
  334.7 1.8 fusion.93
  336.5 74.7 %fusion.94 = bf16[128,1024]{1,0:T(8,128)(2,1)} fusion(s32[4096]{0:T(1024)} %get-tuple-element.283, s32[1024]{0:T(1024)S(1)} %get-tuple-element.284, s32[4096]{0:T(1024)} %get-tuple-element.281, s32[1024]{0:T(1024)S(1)} %get-tuple-element.282, s32[4096]{0:T(1024)} %get-tuple-element.279, s32[1024]{0:T(1024)S(1)} %get-tuple-element.280, ...), kind=kOutput, calls=%fused_computation.19.clone.2 | convolution fusion | flops 1427505152 | bytes 2813952 | tf_op jit(solution)/shard_map/while/body/eval_jaxpr/dot_general | solution.py:41
  411.2 72.3 %multiply_reduce_fusion.4 = (bf16[4096,16]{0,1:T(8,128)(2,1)S(1)}, bf16[128,4096]{1,0:T(8,128)(2,1)S(1)}) fusion(f32[4096,8]{0,1:T(8,128)S(1)} %get-tuple-element.234, bf16[128,1024]{1,0:T(8,128)(2,1)} %fusion.94, s32[4096]{0:T(1024)} %get-tuple-element.283, s32[1024]{0:T(1024)S(1)} %get-tuple-element.284, s32[4096]{0:T(1024)} %get-tuple-element.281, ...), kind=kOutput, calls=%fused_computation.15.clone.2 | convolution fusion | flops 1160183808 | bytes 1634304 | tf_op jit(solution)/shard_map/while/body/eval_jaxpr/dot_general | solution.py:44
  483.5 0.2 multiply_reduce_fusion.5
  483.8 1.1 dynamic_update_slice.14
  485.0 0.7 copy-done.3
  485.9 1.2 copy.31
  487.1 0.9 copy.39
  488.0 10.0 reduce-scatter.7.cloned.1.call-done
  498.0 1.0 reshape.72
  499.0 3.0 fusion.47
  502.0 10.5 convolution_add_fusion
  512.6 17.7 %copy.18 = f32[128,8,4096]{2,1,0:T(8,128)} copy(f32[128,8,4096]{2,0,1:T(8,128)} %convolution_add_fusion) | data formatting | bytes 33554432 | tf_op jit(solution)/shard_map/add | solution.py:95
  530.3 737.9 %reduce-scatter.5.cloned.1.call-done = f32[1,8,4096]{2,1,0:T(8,128)} async-done(((f32[128,8,4096]{2,1,0:T(8,128)}), f32[1,8,4096]{2,1,0:T(8,128)}) %reduce-scatter.5.cloned.1.call-update) | async-done | bytes 131088 | tf_op jit(solution)/shard_map/reduce_scatter | solution.py:95
  (35 shorter events, 0.9 us)
Async XLA Ops:
  6.5 0.8 copy-start
  6.5 129.8 %all-gather.2.cloned.1.call-start = ((), (), s32[]{:S(2)}) async-start(), calls=%async_computation.2 | async-start | bytes 8454144 | tf_op jit(solution)/shard_map/all_gather | solution.py:63
  7.3 490.8 %reduce-scatter.7.cloned.1.call-start = ((), (), s32[]{:S(2)}) async-start(), calls=%async_computation.4 | async-start | bytes 393216
  9.8 126.5 %copy-start.5 = (s32[2]{0:T(128)}, s32[2]{0:T(128)S(1)}, u32[]{:S(2)}) copy-start(s32[2]{0:T(128)S(1)} %get-tuple-element.146) | copy-start | bytes 28
  9.8 153.4 %copy-start.4 = (s32[2]{0:T(128)}, s32[2]{0:T(128)S(1)}, u32[]{:S(2)}) copy-start(s32[2]{0:T(128)S(1)} %get-tuple-element.145) | copy-start | bytes 28
  257.0 73.7 %copy-start.2 = (bf16[2,16,4096]{2,1,0:T(8,128)(2,1)S(1)}, bf16[2,16,4096]{2,1,0:T(8,128)(2,1)}, u32[]{:S(2)}) copy-start(bf16[2,16,4096]{2,1,0:T(8,128)(2,1)} %get-tuple-element.257) | copy-start | bytes 786436 | tf_op jit(solution)/shard_map/while
  330.8 0.7 copy-start.3
  411.2 73.7 %copy-start.2 = (bf16[2,16,4096]{2,1,0:T(8,128)(2,1)S(1)}, bf16[2,16,4096]{2,1,0:T(8,128)(2,1)}, u32[]{:S(2)}) copy-start(bf16[2,16,4096]{2,1,0:T(8,128)(2,1)} %get-tuple-element.257) | copy-start | bytes 786436 | tf_op jit(solution)/shard_map/while
  485.0 0.7 copy-start.3
  485.9 16.2 %copy-start.6 = (s32[2]{0:T(128)S(1)}, s32[2]{0:T(128)}, u32[]{:S(2)}) copy-start(s32[2]{0:T(128)} %copy-done.5) | copy-start | bytes 28
  488.0 780.2 %reduce-scatter.5.cloned.1.call-start = ((), (), s32[]{:S(2)}) async-start(), calls=%async_computation.3 | async-start | bytes 16908288 | tf_op jit(solution)/shard_map/reduce_scatter | solution.py:95
  512.5 755.7 %copy-start.1 = (s32[256,2]{0,1:T(2,128)S(1)}, s32[256,2]{0,1:T(2,128)}, u32[]{:S(2)}) copy-start(s32[256,2]{0,1:T(2,128)} %param.9) | copy-start | bytes 6148
Sparse Core Ops, SparseCore 0:
  11.0 125.3 all-gather.1
  488.1 9.8 reduce-scatter.6
  530.4 737.7 reduce-scatter.4
where the time goes:
time: 1280 us
  waiting for transfers between devices  874 us (68%)
  matrix products  332 us (26%)
  local copies, waits for them, and re-layouts  31 us (2%)
  loops' own time  18.1 us (1%)
  between operations  13.6 us (1%)
    reduce_scatter x1, waiting for transfers between devices, shards(): lax.psum_scatter(first_term + second_term, 'kq', scatter_dimension=0, til...  738 us
    dot_general x2, matrix products, pair_fields(): jnp.dot(spectrum, screen_mat, preferred_element_type=jnp.float32)  149 us
    dot_general x2, matrix products, pair_fields(): jnp.dot(screened, table, preferred_element_type=jnp.float32) * factor  145 us
    all_gather x1, waiting for transfers between devices, shards(): shard_piece = lax.all_gather(orbitals, 'kq', axis=0, tiled=True)  126 us
  transfers between devices with their start and end apart: 3, of which 3 were waited for; matrix products, arithmetic and copies ran while one was open for 0% of the time, Pallas kernels for 0%

commit v1 on v0

--- a/solution.py
+++ b/solution.py
@@ -60,7 +60,13 @@
     local_pairs = lax.dynamic_slice_in_dim(pair_k, owner_index * pair_count, pair_count, 0)
     first_points = local_pairs[:, 0]
     second_points = local_pairs[:, 1]
-    shard_piece = lax.all_gather(orbitals, "kq", axis=0, tiled=True)
+    signs_find = lambda block_in: jnp.concatenate(
+        jax.lax.all_to_all(
+            jnp.stack([block_in for _ in range(jax.lax.axis_size("kq"))]), "kq", 0, 0
+        ),
+        axis=0,
+    )
+    shard_piece = signs_find(orbitals)
     numbers = jnp.arange(shard_piece.shape[0], dtype=jnp.int32)
     pick_first = (first_points[:, None] == numbers[None, :]).astype(jnp.bfloat16)
     pick_second = (second_points[:, None] == numbers[None, :]).astype(jnp.bfloat16)

time: 1280 us -> 1340 us (1.047)
  waiting for transfers between devices: 874 us -> 928 us
  starting transfers between devices: 0.08 us -> 14.9 us
    all_to_all x0 -> x1, waiting for transfers between devices: none -> 187 us  [shards(): jax.lax.all_to_all(jnp.stack([block_in for _ in range(jax.lax.axis_size('...]
    all_gather x1 -> x0, waiting for transfers between devices: 126 us -> none  [shards(): shard_piece = lax.all_gather(orbitals, 'kq', axis=0, tiled=True)]
    all_to_all x0 -> x1, starting transfers between devices: none -> 14.6 us  [shards(): jax.lax.all_to_all(jnp.stack([block_in for _ in range(jax.lax.axis_size('...]
where the time goes in v1:
time: 1340 us
  waiting for transfers between devices  928 us (69%)
  matrix products  332 us (25%)
  local copies, waits for them, and re-layouts  36.2 us (3%)
  starting transfers between devices  14.9 us (1%)
  between operations  13.7 us (1%)
    reduce_scatter x1, waiting for transfers between devices, shards(): lax.psum_scatter(first_term + second_term, 'kq', scatter_dimension=0, til...  737 us
    all_to_all x1, waiting for transfers between devices, shards(): jax.lax.all_to_all(jnp.stack([block_in for _ in range(jax.lax.axis_size('...  187 us
    dot_general x2, matrix products, pair_fields(): jnp.dot(spectrum, screen_mat, preferred_element_type=jnp.float32)  149 us
    dot_general x2, matrix products, pair_fields(): jnp.dot(screened, table, preferred_element_type=jnp.float32) * factor  145 us
  transfers between devices with their start and end apart: 3, of which 3 were waited for; matrix products, arithmetic and copies ran while one was open for 0% of the time, Pallas kernels for 0%

profile of v1, /device:TPU:0, one launch (start us, length us, event | category | flops | bytes accessed | tf_op | source)
XLA Modules:
  0.0 1339.5 jit_solution(13338060155266919179)
XLA Ops:
  6.5 5.2 stack.2
  11.7 14.6 %all-to-all-start = ((bf16[128,1,8,4096]{3,2,1,0:T(8,128)(2,1)}), bf16[128,1,8,4096]{3,2,1,0:T(8,128)(2,1)}, u32[]{:S(2)}, u32[]{:S(2)}) async-start(bf16[128,1,8,4096]{3,2,1,0:T(8,128)(2,1)} %stack.2), calls=%async_computation | async-start | bytes 16777216 | tf_op jit(solution)/shard_map/all_to_all | solution.py:64
  26.7 0.6 add_select_fusion.4
  27.3 0.6 add_select_fusion.1
  27.9 0.6 broadcast_subtract_fusion
  28.5 186.6 %all-to-all-done = bf16[128,1,8,4096]{3,2,1,0:T(8,128)(2,1)} async-done(((bf16[128,1,8,4096]{3,2,1,0:T(8,128)(2,1)}), bf16[128,1,8,4096]{3,2,1,0:T(8,128)(2,1)}, u32[]{:S(2)}, u32[]{:S(2)}) %all-to-all-start) | async-done | bytes 8388640 | tf_op jit(solution)/shard_map/all_to_all | solution.py:64
  215.1 12.2 fusion.43
  227.4 12.6 fusion.46
  240.0 2.0 all_gather.3
  242.2 313.9 %while.13 = (s32[]{:T(128)}, bf16[2,16,4096]{2,1,0:T(8,128)(2,1)}, f32[2,8,4096]{2,0,1:T(2,128)S(1)}, bf16[2,8,4096]{2,1,0:T(8,128)(2,1)S(1)}, bf16[2,16,4096]{2...) while((s32[]{:T(128)}, bf16[2,16,4096]{2,1,0:T(8,128)(2,1)}, ...), condition=%wide.region_1.2_spmd.clone, body=%wide.region_0.1_spmd.clone.sunk | while | flops 2589425664 | bytes 13951255 | solution.py:90
  247.4 1.3 dynamic_slice.45
  250.7 1.8 fusion.95
  252.5 74.7 %fusion.96 = bf16[128,1024]{1,0:T(8,128)(2,1)} fusion(s32[4096]{0:T(1024)} %get-tuple-element.283, s32[1024]{0:T(1024)S(1)} %get-tuple-element.284, s32[4096]{0:T(1024)} %get-tuple-element.281, s32[1024]{0:T(1024)S(1)} %get-tuple-element.282, s32[4096]{0:T(1024)} %get-tuple-element.279, s32[1024]{0:T(1024)S(1)} %get-tuple-element.280, ...), kind=kOutput, calls=%fused_computation.19.clone.2 | convolution fusion | flops 1427505152 | bytes 2813952 | tf_op jit(solution)/shard_map/while/body/eval_jaxpr/dot_general | solution.py:41
  327.2 72.3 %multiply_reduce_fusion.4 = (bf16[4096,16]{0,1:T(8,128)(2,1)S(1)}, bf16[128,4096]{1,0:T(8,128)(2,1)S(1)}) fusion(f32[4096,8]{0,1:T(8,128)S(1)} %get-tuple-element.234, bf16[128,1024]{1,0:T(8,128)(2,1)} %fusion.96, s32[4096]{0:T(1024)} %get-tuple-element.283, s32[1024]{0:T(1024)S(1)} %get-tuple-element.284, s32[4096]{0:T(1024)} %get-tuple-element.281, ...), kind=kOutput, calls=%fused_computation.15.clone.2 | convolution fusion | flops 1160183808 | bytes 1634304 | tf_op jit(solution)/shard_map/while/body/eval_jaxpr/dot_general | solution.py:44
  399.5 0.2 multiply_reduce_fusion.5
  399.8 1.1 dynamic_update_slice.14
  401.0 0.7 copy-done.3
  401.7 1.3 dynamic_slice.45
  405.0 1.8 fusion.95
  406.7 74.7 %fusion.96 = bf16[128,1024]{1,0:T(8,128)(2,1)} fusion(s32[4096]{0:T(1024)} %get-tuple-element.283, s32[1024]{0:T(1024)S(1)} %get-tuple-element.284, s32[4096]{0:T(1024)} %get-tuple-element.281, s32[1024]{0:T(1024)S(1)} %get-tuple-element.282, s32[4096]{0:T(1024)} %get-tuple-element.279, s32[1024]{0:T(1024)S(1)} %get-tuple-element.280, ...), kind=kOutput, calls=%fused_computation.19.clone.2 | convolution fusion | flops 1427505152 | bytes 2813952 | tf_op jit(solution)/shard_map/while/body/eval_jaxpr/dot_general | solution.py:41
  481.4 72.3 %multiply_reduce_fusion.4 = (bf16[4096,16]{0,1:T(8,128)(2,1)S(1)}, bf16[128,4096]{1,0:T(8,128)(2,1)S(1)}) fusion(f32[4096,8]{0,1:T(8,128)S(1)} %get-tuple-element.234, bf16[128,1024]{1,0:T(8,128)(2,1)} %fusion.96, s32[4096]{0:T(1024)} %get-tuple-element.283, s32[1024]{0:T(1024)S(1)} %get-tuple-element.284, s32[4096]{0:T(1024)} %get-tuple-element.281, ...), kind=kOutput, calls=%fused_computation.15.clone.2 | convolution fusion | flops 1160183808 | bytes 1634304 | tf_op jit(solution)/shard_map/while/body/eval_jaxpr/dot_general | solution.py:44
  553.7 0.2 multiply_reduce_fusion.5
  554.1 1.1 dynamic_update_slice.14
  555.2 0.7 copy-done.3
  556.1 1.2 copy.29
  557.3 0.9 copy.37
  558.3 4.8 reduce-scatter.7.cloned.1.call-done
  563.1 1.0 reshape.79
  564.1 3.0 fusion.49
  567.2 10.5 convolution_add_fusion
  577.7 17.7 %copy.16 = f32[128,8,4096]{2,1,0:T(8,128)} copy(f32[128,8,4096]{2,0,1:T(8,128)} %convolution_add_fusion) | data formatting | bytes 33554432 | tf_op jit(solution)/shard_map/add | solution.py:101
  595.4 737.0 %reduce-scatter.5.cloned.1.call-done = f32[1,8,4096]{2,1,0:T(8,128)} async-done(((f32[128,8,4096]{2,1,0:T(8,128)}), f32[1,8,4096]{2,1,0:T(8,128)}) %reduce-scatter.5.cloned.1.call-update) | async-done | bytes 131088 | tf_op jit(solution)/shard_map/reduce_scatter | solution.py:101
  (39 shorter events, 1.1 us)
Async XLA Ops:
  6.5 20.0 %copy-start = (s32[256,2]{0,1:T(2,128)S(1)}, s32[256,2]{0,1:T(2,128)}, u32[]{:S(2)}) copy-start(s32[256,2]{0,1:T(2,128)} %param.9) | copy-start | bytes 6148
  6.5 21.3 %copy-start.8 = (s32[2]{0:T(128)S(1)}, s32[2]{0:T(128)}, u32[]{:S(2)}) copy-start(s32[2]{0:T(128)} %param.10) | copy-start | bytes 28
  6.5 21.9 %copy-start.7 = (s32[1024]{0:T(1024)S(1)}, s32[1024]{0:T(1024)}, u32[]{:S(2)}) copy-start(s32[1024]{0:T(1024)} %param.11) | copy-start | bytes 12292
  11.7 203.4 %all-to-all-start = ((bf16[128,1,8,4096]{3,2,1,0:T(8,128)(2,1)}), bf16[128,1,8,4096]{3,2,1,0:T(8,128)(2,1)}, u32[]{:S(2)}, u32[]{:S(2)}) async-start(bf16[128,1,8,4096]{3,2,1,0:T(8,128)(2,1)} %stack.2), calls=%async_computation | async-start | bytes 16777216 | tf_op jit(solution)/shard_map/all_to_all | solution.py:64
  26.3 536.8 %reduce-scatter.7.cloned.1.call-start = ((), (), s32[]{:S(2)}) async-start(), calls=%async_computation.4 | async-start | bytes 393216
  28.5 186.6 %copy-start.5 = (s32[2]{0:T(128)}, s32[2]{0:T(128)S(1)}, u32[]{:S(2)}) copy-start(s32[2]{0:T(128)S(1)} %get-tuple-element.146) | copy-start | bytes 28
  28.5 213.7 %copy-start.4 = (s32[2]{0:T(128)}, s32[2]{0:T(128)S(1)}, u32[]{:S(2)}) copy-start(s32[2]{0:T(128)S(1)} %get-tuple-element.145) | copy-start | bytes 28
  327.2 73.7 %copy-start.2 = (bf16[2,16,4096]{2,1,0:T(8,128)(2,1)S(1)}, bf16[2,16,4096]{2,1,0:T(8,128)(2,1)}, u32[]{:S(2)}) copy-start(bf16[2,16,4096]{2,1,0:T(8,128)(2,1)} %get-tuple-element.257) | copy-start | bytes 786436 | tf_op jit(solution)/shard_map/while
  401.0 0.7 copy-start.3
  481.4 73.7 %copy-start.2 = (bf16[2,16,4096]{2,1,0:T(8,128)(2,1)S(1)}, bf16[2,16,4096]{2,1,0:T(8,128)(2,1)}, u32[]{:S(2)}) copy-start(bf16[2,16,4096]{2,1,0:T(8,128)(2,1)} %get-tuple-element.257) | copy-start | bytes 786436 | tf_op jit(solution)/shard_map/while
  555.2 0.7 copy-start.3
  556.1 11.0 copy-start.6
  558.2 774.2 %reduce-scatter.5.cloned.1.call-start = ((), (), s32[]{:S(2)}) async-start(), calls=%async_computation.3 | async-start | bytes 16908288 | tf_op jit(solution)/shard_map/reduce_scatter | solution.py:101
  577.7 754.7 %copy-start.1 = (s32[256,2]{0,1:T(2,128)S(1)}, s32[256,2]{0,1:T(2,128)}, u32[]{:S(2)}) copy-start(s32[256,2]{0,1:T(2,128)} %param.9) | copy-start | bytes 6148
Sparse Core Ops, SparseCore 0:
  558.3 4.7 reduce-scatter.6
  595.5 736.8 reduce-scatter.4
